TPU v7x, 32 devices: a whole 2x2x4 slice. The times are simulated.
32 devices in a mesh: row: 4 (over y, x), col: 8 (over z, core).
Axes of the slice: x: 2, y: 2, z: 4, core: 2. Of those that a mesh axis runs over, the one named last changes fastest.
Arguments:
- node_features: bfloat16 [2048, 128, 512], P(('row', 'col')), may hold values from -6 to 6
- node_counts: int32 [2048], P(('row', 'col')), may hold values from 16 to 128, as said below
- edge_list: int32 [2048, 2, 256], P(('row', 'col')), may hold values from 0 to 128, as said below
- readout_ids: int32 [2048], P(('row', 'col')), may hold values from 0 to 255
- live_graphs: int32 [32], P(('row', 'col')), may hold values from 1 to 64, as said below
- self_weight: float32 [1], replicated, may hold values from 0.5 to 1.5
- w_first: bfloat16 [512, 512], replicated, may hold values from -0.25 to 0.25
- b_first: float32 [512], replicated, may hold values from -3 to 3
- w_second: bfloat16 [512, 512], replicated, may hold values from -0.25 to 0.25
- b_second: float32 [512], replicated, may hold values from -3 to 3
- w_third: bfloat16 [512, 512], replicated, may hold values from -0.25 to 0.25
- b_third: float32 [512], replicated, may hold values from -3 to 3
Outputs:
- node_out: bfloat16 [1024, 128, 512], P(('row', 'col'))
- readout: float32 [256, 512], P(('row', 'col'))
Inputs may be any that keep to these rules, and one draw needn't show every extreme that they name: `live_graphs`: the entries sum to 1024, and at least one equals 64. `node_counts`: node slots 0 to count - 1 of a graph are live; the rest of its block is padding. `edge_list`: each edge slot holds two node indices below its graph's node count, or 128 in both rows for an unused slot.
All inputs are finite; a program needn't handle non-finite values.
Results may differ from a plain program's by a relative error of at most 0.0058.
Values may be sent and summed in bfloat16 or wider, within the bound.
A program may use at most 128 MiB of HBM per device.

v0:
```python
import jax
import jax.numpy as jnp
from jax import lax
from jax.sharding import PartitionSpec as P

G_DEV = 32
READ_DEV = 8


def blend_nodes(features, edge_slots, self_weight):
    node_index = lax.broadcasted_iota(jnp.int32, (1, 1, features.shape[1]), 2)
    sources = (edge_slots[:, 0, :, None] == node_index).astype(jnp.bfloat16)
    targets = (edge_slots[:, 1, :, None] == node_index).astype(jnp.bfloat16)
    adjacency = jnp.einsum(
        "gek,gel->gkl", targets, sources, preferred_element_type=jnp.float32
    ).astype(jnp.bfloat16)
    neighbour = jnp.einsum("gkl,glh->gkh", adjacency, features, preferred_element_type=jnp.float32)
    return (self_weight[0] * features.astype(jnp.float32) + neighbour).astype(jnp.bfloat16)


def perceptron(blended, weights):
    w_first, b_first, w_second, b_second, w_third, b_third = weights
    flat_rows = blended.reshape(-1, blended.shape[-1])
    hidden_one = jax.nn.relu(
        jnp.dot(flat_rows, w_first, preferred_element_type=jnp.float32) + b_first
    ).astype(jnp.bfloat16)
    hidden_two = jax.nn.relu(
        jnp.dot(hidden_one, w_second, preferred_element_type=jnp.float32) + b_second
    ).astype(jnp.bfloat16)
    result = jnp.dot(hidden_two, w_third, preferred_element_type=jnp.float32) + b_third
    return result.reshape(blended.shape)


def arrival_index(slot_tags):
    wanted = lax.broadcasted_iota(jnp.int32, (G_DEV, slot_tags.shape[0]), 0)
    places = lax.broadcasted_iota(jnp.int32, (G_DEV, slot_tags.shape[0]), 1)
    return jnp.sum(jnp.where(slot_tags[None, :] == wanted, places, 0), axis=1)


def readout_terms(graph_ids, pooled, row_count):
    id_keys = lax.broadcasted_iota(jnp.int32, (row_count, graph_ids.shape[0]), 0)
    members = (id_keys == graph_ids[None, :]).astype(jnp.float32)
    return jnp.dot(
        members, pooled, precision=lax.Precision.HIGHEST, preferred_element_type=jnp.float32
    )


def body(
    node_features,
    node_counts,
    edge_list,
    readout_ids,
    live_graphs,
    self_weight,
    w_first,
    b_first,
    w_second,
    b_second,
    w_third,
    b_third,
):
    weights = (w_first, b_first, w_second, b_second, w_third, b_third)
    devices = lax.axis_size(("row", "col"))
    capacity = node_features.shape[0]
    bucket = (capacity + devices - 1) // devices
    own_count = live_graphs[0]
    every_count = lax.all_gather(live_graphs, ("row", "col"), axis=0, tiled=True)
    position = lax.broadcasted_iota(jnp.int32, (devices,), 0)
    offset = jnp.sum(jnp.where(position < lax.axis_index(("row", "col")), every_count, 0))
    targets = lax.broadcasted_iota(jnp.int32, (devices * bucket,), 0)
    dest_device = targets // bucket
    within = (dest_device - offset) % devices + targets % bucket * devices
    sending_ok = within < own_count
    slot_tags = jnp.where(sending_ok, (offset + within) // devices, G_DEV)
    picked = jnp.minimum(within, capacity - 1)
    node_index = lax.broadcasted_iota(jnp.int32, (1, node_features.shape[1]), 1)
    blended = blend_nodes(node_features, edge_list, self_weight)
    live_nodes = node_index < node_counts[:, None]
    results = jnp.where(live_nodes[:, :, None], perceptron(blended, weights), 0.0).astype(
        jnp.bfloat16
    )
    pooled = jnp.sum(results.astype(jnp.float32), axis=1) / node_counts[:, None].astype(jnp.float32)
    slot_live = lax.broadcasted_iota(jnp.int32, (capacity,), 0) < own_count
    graph_ids = jnp.where(slot_live, readout_ids, -1)
    arrived, arrived_tags = (
        lax.all_to_all(results[picked], ("row", "col"), split_axis=0, concat_axis=0, tiled=True),
        lax.all_to_all(slot_tags, ("row", "col"), split_axis=0, concat_axis=0, tiled=True),
    )
    node_out = arrived[arrival_index(arrived_tags)]
    totals = lax.psum(readout_terms(graph_ids, pooled, READ_DEV * devices), ("row", "col"))
    readout = lax.dynamic_slice_in_dim(
        totals, lax.axis_index(("row", "col")) * READ_DEV, READ_DEV, 0
    )
    return (node_out, readout)


def solution(mesh):
    in_specs = (
        P(("row", "col"), None, None),
        P(("row", "col")),
        P(("row", "col"), None, None),
        P(("row", "col")),
        P(("row", "col")),
        P(),
        P(),
        P(),
        P(),
        P(),
        P(),
        P(),
    )
    out_specs = (P(("row", "col"), None, None), P(("row", "col"), None))
    return jax.shard_map(body, mesh=mesh, in_specs=in_specs, out_specs=out_specs, check_vma=False)
```

profile of v0, /device:TPU:0, one launch (start us, length us, event | category | flops | bytes accessed | tf_op | source)
XLA Modules:
  0.0 323.4 jit_solution(11251081128402884339)
XLA Ops:
  7.2 0.0 copy-start
  7.9 0.1 dynamic-update-slice
  8.0 41.9 %all-reduce = s32[32]{0:T(128)S(1)} all-reduce(s32[32]{0:T(128)S(1)} %dynamic-update-slice), channel_id=1, replica_groups=mesh['row'=4,'col'=8] {'row','col'}, use_global_device_ids=true, to_apply=%add | all-reduce | flops 32 | bytes 256
  50.0 0.6 fusion.15
  50.6 1.4 compare_select_fusion.2
  52.0 4.4 %all-to-all-start.1 = ((s32[32,2,1]{1,2,0:T(1,128)}), s32[32,2,1]{1,2,0:T(1,128)S(1)}, u32[]{:S(2)}, u32[]{:S(2)}) async-start(s32[32,2,1]{1,2,0:T(1,128)} %compare_select_fusion.2), calls=%async_computation.1 | async-start | bytes 32768 | tf_op jit(solution)/shard_map/all_to_all | solution.py:87
  56.4 0.7 fusion.17
  57.1 1.1 fusion.20
  58.8 0.7 iota_compare_fusion.14
  59.6 0.0 copy-start.4
  59.6 12.6 %add_convert_fusion = bf16[64,128,512]{2,1,0:T(8,128)(2,1)} fusion(bf16[64,128,512]{2,1,0:T(8,128)(2,1)} %param.12, f32[]{:T(128)} %bitcast.24, s32[64,256]{1,0:T(8,128)S(1)} %get-tuple-element.6, s32[64,256]{1,0:T(8,128)S(1)} %get-tuple-element.7), kind=kOutput, calls=%fused_computation.6 | convolution fusion | flops 1632632832 | bytes 16908292 | tf_op jit(solution)/shard_map/gkl,glh->gkh/dot_general | solution.py:17
  72.2 0.0 copy-done
  72.2 0.0 copy-done.4
  72.2 0.0 copy-start.2
  72.2 0.0 copy-start.3
  72.2 0.0 copy-start.5
  72.2 0.0 copy-start.6
  72.2 10.2 %maximum_convert_fusion.1 = bf16[8192,512]{1,0:T(8,128)(2,1)} fusion(bf16[8192,512]{1,0:T(8,128)(2,1)} %bitcast.25, bf16[512,512]{1,0:T(8,128)(2,1)S(1)} %copy-done, f32[512]{0:T(512)S(1)} %copy-done.4), kind=kOutput, calls=%fused_computation.5 | convolution fusion | flops 4307550208 | bytes 17303552 | tf_op jit(solution)/shard_map/dot_general | solution.py:25
  82.4 0.0 copy-done.2
  82.4 0.0 copy-done.3
  82.4 0.0 copy-done.5
  82.4 0.0 copy-done.6
  82.5 13.3 %convolution_add_fusion = bf16[8192,512]{1,0:T(8,128)(2,1)} fusion(bf16[512,512]{1,0:T(8,128)(2,1)S(1)} %copy-done.2, f32[512]{0:T(512)S(1)} %copy-done.5, bf16[8192,512]{1,0:T(8,128)(2,1)} %maximum_convert_fusion.1, bf16[512,512]{1,0:T(8,128)(2,1)S(1)} %copy-done.3, f32[512]{0:T(512)S(1)} %copy-done.6), kind=kOutput, calls=%fused_computation.7 | convolution fusion | flops 8610906112 | bytes 17829888 | tf_op jit(solution)/shard_map/dot_general | solution.py:30
  95.7 8.3 %convert_reduce_fusion = (f32[64,512]{1,0:T(8,128)S(1)}, bf16[64,128,512]{2,1,0:T(8,128)(2,1)}) fusion(pred[64,128]{1,0:T(8,128)(4,1)S(1)} %iota_compare_fusion.14, bf16[8192,512]{1,0:T(8,128)(2,1)} %convolution_add_fusion), kind=kLoop, calls=%fused_computation.2 | loop fusion | flops 12550144 | bytes 16916480 | tf_op jit(solution)/shard_map/reduce_sum | solution.py:82
  104.1 8.9 %gather_fusion = bf16[64,128,512]{2,1,0:T(8,128)(2,1)} fusion(bf16[64,128,512]{2,1,0:T(8,128)(2,1)} %get-tuple-element.3, s32[1024]{0:T(1024)S(1)} %pad_clamp_fusion.1), kind=kCustom, calls=%fused_computation | custom fusion | bytes 16777472 | tf_op jit(solution)/shard_map/gather | solution.py:86
  113.0 0.0 copy-start.1
  113.0 0.0 copy-start.7
  113.0 0.0 all-to-all-done.1
  113.0 6.0 %all-to-all-start = ((bf16[64,128,512]{2,1,0:T(8,128)(2,1)}), bf16[64,128,512]{2,1,0:T(8,128)(2,1)}, u32[]{:S(2)}, u32[]{:S(2)}) async-start(bf16[64,128,512]{2,1,0:T(8,128)(2,1)} %gather_fusion), calls=%async_computation | async-start | bytes 16777216 | tf_op jit(solution)/shard_map/all_to_all | solution.py:86
  119.0 0.0 all-reduce.3.cloned.1.call-start
  119.0 0.0 copy-done.1
  119.0 0.0 copy-done.7
  119.0 1.2 fusion.4
  120.3 0.0 all-reduce.3.cloned.1.call-update
  120.3 0.5 broadcast.399
  120.8 0.7 reduce.3
  121.5 0.1 eq.59
  121.6 0.1 select_reduce_fusion
  121.8 173.9 %all-reduce.3.cloned.1.call-done = f32[256,512]{1,0:T(8,128)} async-done(((f32[256,512]{1,0:T(8,128)}), f32[256,512]{1,0:T(8,128)}) %all-reduce.3.cloned.1.call-update) | async-done | bytes 524304 | tf_op jit(solution)/shard_map/psum | solution.py:90
  295.6 1.3 constant_dynamic-slice_fusion
  297.0 13.4 %all-to-all-done = bf16[64,128,512]{2,1,0:T(8,128)(2,1)} async-done(((bf16[64,128,512]{2,1,0:T(8,128)(2,1)}), bf16[64,128,512]{2,1,0:T(8,128)(2,1)}, u32[]{:S(2)}, u32[]{:S(2)}) %all-to-all-start) | async-done | bytes 8388640 | tf_op jit(solution)/shard_map/all_to_all | solution.py:86
  310.4 6.2 %gather_fusion.1 = bf16[32,128,512]{2,1,0:T(8,128)(2,1)} fusion(bf16[64,128,512]{2,1,0:T(8,128)(2,1)} %all-to-all-done, s32[1024]{0:T(1024)S(1)} %pad_clamp_fusion), kind=kCustom, calls=%fused_computation.1 | custom fusion | bytes 8388736 | tf_op jit(solution)/shard_map/gather | solution.py:89
  (7 shorter events, 0.0 us)
Async XLA Ops:
  7.2 65.0 %copy-start = (bf16[512,512]{1,0:T(8,128)(2,1)S(1)}, bf16[512,512]{1,0:T(8,128)(2,1)}, u32[]{:S(2)}) copy-start(bf16[512,512]{1,0:T(8,128)(2,1)} %param.18) | copy-start | bytes 1572868
  52.0 61.0 %all-to-all-start.1 = ((s32[32,2,1]{1,2,0:T(1,128)}), s32[32,2,1]{1,2,0:T(1,128)S(1)}, u32[]{:S(2)}, u32[]{:S(2)}) async-start(s32[32,2,1]{1,2,0:T(1,128)} %compare_select_fusion.2), calls=%async_computation.1 | async-start | bytes 32768 | tf_op jit(solution)/shard_map/all_to_all | solution.py:87
  59.6 12.6 %copy-start.4 = (f32[512]{0:T(512)S(1)}, f32[512]{0:T(512)}, u32[]{:S(2)}) copy-start(f32[512]{0:T(512)} %param.19) | copy-start | bytes 6148
  72.2 10.3 %copy-start.2 = (bf16[512,512]{1,0:T(8,128)(2,1)S(1)}, bf16[512,512]{1,0:T(8,128)(2,1)}, u32[]{:S(2)}) copy-start(bf16[512,512]{1,0:T(8,128)(2,1)} %param.22) | copy-start | bytes 1572868
  72.2 10.3 %copy-start.3 = (bf16[512,512]{1,0:T(8,128)(2,1)S(1)}, bf16[512,512]{1,0:T(8,128)(2,1)}, u32[]{:S(2)}) copy-start(bf16[512,512]{1,0:T(8,128)(2,1)} %param.20) | copy-start | bytes 1572868
  72.2 10.3 %copy-start.5 = (f32[512]{0:T(512)S(1)}, f32[512]{0:T(512)}, u32[]{:S(2)}) copy-start(f32[512]{0:T(512)} %param.23) | copy-start | bytes 6148
  72.2 10.3 %copy-start.6 = (f32[512]{0:T(512)S(1)}, f32[512]{0:T(512)}, u32[]{:S(2)}) copy-start(f32[512]{0:T(512)} %param.21) | copy-start | bytes 6148
  113.0 6.0 %copy-start.1 = (s32[64]{0:T(128)S(1)}, s32[64]{0:T(128)}, u32[]{:S(2)}) copy-start(s32[64]{0:T(128)} %param.13) | copy-start | bytes 772
  113.0 6.1 %copy-start.7 = (s32[64]{0:T(128)S(1)}, s32[64]{0:T(128)}, u32[]{:S(2)}) copy-start(s32[64]{0:T(128)} %param.15) | copy-start | bytes 772
  113.0 197.4 %all-to-all-start = ((bf16[64,128,512]{2,1,0:T(8,128)(2,1)}), bf16[64,128,512]{2,1,0:T(8,128)(2,1)}, u32[]{:S(2)}, u32[]{:S(2)}) async-start(bf16[64,128,512]{2,1,0:T(8,128)(2,1)} %gather_fusion), calls=%async_computation | async-start | bytes 16777216 | tf_op jit(solution)/shard_map/all_to_all | solution.py:86
  119.0 176.7 %all-reduce.3.cloned.1.call-start = ((), (), s32[]{:S(2)}) async-start(), calls=%async_computation.2 | async-start | bytes 1048576 | tf_op jit(solution)/shard_map/psum | solution.py:90
Sparse Core Ops, SparseCore 0:
  125.6 169.9 all-reduce.2
where the time goes:
time: 324 us; the launch traced here: 323 us
  waiting for transfers between devices  187 us (58%)
  blocking collectives  41.9 us (13%)
  matrix products  37.3 us (12%)
  local copies, waits for them, and re-layouts  18.3 us (6%)
  between operations  15.6 us (5%)
  other arithmetic  12.6 us (4%)
  starting transfers between devices  10.4 us (3%)
    psum x1, waiting for transfers between devices, body(): lax.psum(readout_terms(graph_ids, pooled, READ_DEV * devices), ('row', 'c...  174 us
    unnamed x1, blocking collectives  41.9 us
    all_to_all x1, waiting for transfers between devices, body(): lax.all_to_all(results[picked], ('row', 'col'), split_axis=0, concat_axis...  13.4 us
    dot_general x1, matrix products, perceptron(): jnp.dot(hidden_two, w_third, preferred_element_type=jnp.float32) + b_third  13.3 us
    dot_general x1, matrix products, blend_nodes(): jnp.einsum('gkl,glh->gkh', adjacency, features, preferred_element_type=jn...  12.6 us
    dot_general x1, matrix products, perceptron(): jnp.dot(flat_rows, w_first, preferred_element_type=jnp.float32) + b_first  10.2 us
    gather x1, local copies, waits for them, and re-layouts, body(): results[picked]  8.91 us
    reduce_sum x1, other arithmetic, body(): jnp.sum(results.astype(jnp.float32), axis=1)  8.33 us
  transfers between devices with their start and end apart: 3, of which 2 were waited for; matrix products, arithmetic and copies ran while one was open for 18% of the time, Pallas kernels for 0%

commit v1 on v0

v1 whole, which is shorter than its diff:
```python
import functools

import jax
import jax.numpy as jnp
from jax import lax
from jax.experimental import pallas as pl
from jax.experimental.pallas import tpu as pltpu
from jax.sharding import PartitionSpec as P

MESH = pl.DeviceIdType.MESH
VMEM = pl.BlockSpec(memory_space=pltpu.VMEM)
SMEM = pl.BlockSpec(memory_space=pltpu.SMEM)


def partners(step, sizes):
    rows, cols = sizes
    row, col = lax.axis_index("row"), lax.axis_index("col")
    by_row, by_col = step // cols, (step % cols) * 3 % cols
    to_row, to_col = (row + by_row) % rows, (col + by_col) % cols
    from_row, from_col = (row + rows - by_row) % rows, (col + cols - by_col) % cols
    return (to_row, to_col), to_row * cols + to_col, from_row * cols + from_col


def greet(sizes):
    barrier = pltpu.get_barrier_semaphore()
    devices = sizes[0] * sizes[1]

    def signal(step, carry):
        where, _, _ = partners(step, sizes)
        pl.semaphore_signal(barrier, inc=1, device_id=where, device_id_type=MESH)
        return carry

    lax.fori_loop(1, devices, signal, 0)
    return barrier


def gather_kernel(sizes, own_ref, all_ref, send_sem, recv_sem):
    devices = sizes[0] * sizes[1]
    me = lax.axis_index("row") * sizes[1] + lax.axis_index("col")
    barrier = greet(sizes)
    all_ref[me] = own_ref[0]
    pl.semaphore_wait(barrier, devices - 1)

    def copy(step, slot):
        where, _, _ = partners(step, sizes)
        return pltpu.make_async_remote_copy(
            src_ref=own_ref.at[0],
            dst_ref=all_ref.at[slot],
            send_sem=send_sem.at[step],
            recv_sem=recv_sem.at[step],
            device_id=where,
            device_id_type=MESH,
        )

    def send(step, carry):
        copy(step, me).start()
        return carry

    def finish(step, carry):
        _, _, source = partners(step, sizes)
        copy(step, me).wait_send()
        copy(step, source).wait_recv()
        return carry

    lax.fori_loop(1, devices, send, 0)
    lax.fori_loop(1, devices, finish, 0)


def gather_counts(live_graphs, sizes):
    devices = sizes[0] * sizes[1]
    own = jnp.broadcast_to(live_graphs.reshape(1, 1, 1), (1, 1, 128))
    every = pl.pallas_call(
        functools.partial(gather_kernel, sizes),
        out_shape=jax.ShapeDtypeStruct((devices, 1, 128), jnp.int32),
        in_specs=[VMEM],
        out_specs=VMEM,
        scratch_shapes=[
            pltpu.SemaphoreType.DMA((devices,)),
            pltpu.SemaphoreType.DMA((devices,)),
        ],
        compiler_params=pltpu.CompilerParams(collective_id=0, has_side_effects=True),
        name="gather_counts",
    )(own)
    return every[:, 0, 0]


def layer_kernel(
    sizes,
    bucket,
    picked_ref,
    counts_ref,
    arrival_ref,
    weight_ref,
    features_ref,
    edges_ref,
    ids_ref,
    w_first_ref,
    b_first_ref,
    w_second_ref,
    b_second_ref,
    w_third_ref,
    b_third_ref,
    out_ref,
    readout_ref,
    sent,
    arrived,
    pooled,
    terms,
    terms_in,
    send_sem,
    recv_sem,
    terms_send_sem,
    terms_recv_sem,
):
    devices = sizes[0] * sizes[1]
    read_rows = readout_ref.shape[0]
    block, hidden = features_ref.shape[1:]
    me = lax.axis_index("row") * sizes[1] + lax.axis_index("col")
    barrier = greet(sizes)

    def graph_copy(step, target, slot):
        where, _, _ = partners(step, sizes)
        return pltpu.make_async_remote_copy(
            src_ref=sent.at[target],
            dst_ref=arrived.at[slot],
            send_sem=send_sem.at[step],
            recv_sem=recv_sem.at[step],
            device_id=where,
            device_id_type=MESH,
        )

    def terms_copy(step, target, slot):
        where, _, _ = partners(step, sizes)
        return pltpu.make_async_remote_copy(
            src_ref=terms.at[target],
            dst_ref=terms_in.at[slot],
            send_sem=terms_send_sem.at[step],
            recv_sem=terms_recv_sem.at[step],
            device_id=where,
            device_id_type=MESH,
        )

    node_rows = lax.broadcasted_iota(jnp.int32, (block, edges_ref.shape[2]), 0)
    node_index = lax.broadcasted_iota(jnp.int32, (block, hidden), 0)

    def compute(target, store):
        blends = []
        for j in range(bucket):
            graph = picked_ref[target * bucket + j]
            features = features_ref[graph]
            edges = edges_ref[graph]
            sources = (node_rows == edges[0:1, :]).astype(jnp.float32).astype(jnp.bfloat16)
            targets = (node_rows == edges[1:2, :]).astype(jnp.float32).astype(jnp.bfloat16)
            adjacency = lax.dot_general(
                targets,
                sources,
                (((1,), (1,)), ((), ())),
                preferred_element_type=jnp.float32,
            ).astype(jnp.bfloat16)
            neighbour = jnp.dot(adjacency, features, preferred_element_type=jnp.float32)
            blends.append(
                (weight_ref[0] * features.astype(jnp.float32) + neighbour).astype(jnp.bfloat16)
            )
        blended = jnp.concatenate(blends, axis=0) if bucket > 1 else blends[0]
        hidden_one = jnp.maximum(
            jnp.dot(blended, w_first_ref[...], preferred_element_type=jnp.float32)
            + b_first_ref[...],
            0.0,
        ).astype(jnp.bfloat16)
        hidden_two = jnp.maximum(
            jnp.dot(hidden_one, w_second_ref[...], preferred_element_type=jnp.float32)
            + b_second_ref[...],
            0.0,
        ).astype(jnp.bfloat16)
        result = (
            jnp.dot(hidden_two, w_third_ref[...], preferred_element_type=jnp.float32)
            + b_third_ref[...]
        )
        for j in range(bucket):
            count = counts_ref[target * bucket + j]
            rows = jnp.where(node_index < count, result[j * block : (j + 1) * block], 0.0)
            rows = rows.astype(jnp.bfloat16)
            store(j, rows)
            total = jnp.sum(rows.astype(jnp.float32), axis=0, keepdims=True)
            pooled[target * bucket + j] = total / jnp.full((1, hidden), count).astype(jnp.float32)

    pl.semaphore_wait(barrier, devices - 1)

    def compute_and_send(step, carry):
        _, target, _ = partners(step, sizes)

        def store(j, rows):
            sent[target, j] = rows

        compute(target, store)
        graph_copy(step, target, me).start()
        return carry

    lax.fori_loop(1, devices, compute_and_send, 0)

    def store_own(j, rows):
        arrived[me, j] = rows

    compute(me, store_own)

    slots = devices * bucket
    keys = lax.broadcasted_iota(jnp.int32, (devices * read_rows, slots), 0)
    members = (keys == ids_ref[...]).astype(jnp.float32)
    all_terms = jnp.dot(
        members,
        pooled[...].reshape(slots, hidden),
        precision=lax.Precision.HIGHEST,
        preferred_element_type=jnp.float32,
    )
    terms[...] = all_terms.reshape(devices, read_rows, hidden)

    def send_terms(step, carry):
        _, target, _ = partners(step, sizes)
        terms_copy(step, target, me).start()
        return carry

    lax.fori_loop(1, devices, send_terms, 0)
    terms_in[me] = terms[me]

    def finish(step, carry):
        _, target, source = partners(step, sizes)
        graph_copy(step, target, me).wait_send()
        graph_copy(step, target, source).wait_recv()
        terms_copy(step, target, me).wait_send()
        terms_copy(step, target, source).wait_recv()
        return carry

    lax.fori_loop(1, devices, finish, 0)
    readout_ref[...] = jnp.sum(terms_in[...], axis=0)

    def place(slot, carry):
        which = arrival_ref[slot]
        out_ref[slot] = arrived[which // bucket, which % bucket]
        return carry

    lax.fori_loop(0, out_ref.shape[0], place, 0)


def body(
    sizes,
    node_features,
    node_counts,
    edge_list,
    readout_ids,
    live_graphs,
    self_weight,
    w_first,
    b_first,
    w_second,
    b_second,
    w_third,
    b_third,
):
    devices = sizes[0] * sizes[1]
    capacity, block, hidden = node_features.shape
    graphs_out = capacity // 2
    read_rows = 8
    bucket = (capacity + devices - 1) // devices
    own_count = live_graphs[0]
    me = lax.axis_index(("row", "col"))
    every_count = gather_counts(live_graphs, sizes)
    inclusive = jnp.cumsum(every_count)
    offsets = inclusive - every_count
    offset = offsets[me]
    slots = lax.broadcasted_iota(jnp.int32, (devices * bucket,), 0)
    within = (slots // bucket - offset) % devices + slots % bucket * devices
    picked = jnp.minimum(within, capacity - 1)
    counts = node_counts[picked]
    graph_ids = jnp.where(within < own_count, readout_ids[picked], -1)
    number = lax.broadcasted_iota(jnp.int32, (graphs_out,), 0) * devices + me
    passed = (inclusive[None, :] <= number[:, None]).astype(jnp.int32)
    source = jnp.sum(passed, axis=1)
    start = jnp.sum(passed * every_count[None, :], axis=1)
    arrival = source * bucket + (number - start) // devices
    return pl.pallas_call(
        functools.partial(layer_kernel, sizes, bucket),
        out_shape=(
            jax.ShapeDtypeStruct((graphs_out, block, hidden), jnp.bfloat16),
            jax.ShapeDtypeStruct((read_rows, hidden), jnp.float32),
        ),
        in_specs=[SMEM] * 4 + [VMEM] * 9,
        out_specs=(VMEM, VMEM),
        scratch_shapes=[
            pltpu.VMEM((devices, bucket, block, hidden), jnp.bfloat16),
            pltpu.VMEM((devices, bucket, block, hidden), jnp.bfloat16),
            pltpu.VMEM((devices * bucket, 1, hidden), jnp.float32),
            pltpu.VMEM((devices, read_rows, hidden), jnp.float32),
            pltpu.VMEM((devices, read_rows, hidden), jnp.float32),
            pltpu.SemaphoreType.DMA((devices,)),
            pltpu.SemaphoreType.DMA((devices,)),
            pltpu.SemaphoreType.DMA((devices,)),
            pltpu.SemaphoreType.DMA((devices,)),
        ],
        compiler_params=pltpu.CompilerParams(
            collective_id=1, has_side_effects=True, vmem_limit_bytes=60 * 1024 * 1024
        ),
        name="gin_layer",
    )(
        picked,
        counts,
        arrival,
        self_weight,
        node_features,
        edge_list,
        graph_ids.reshape(1, -1),
        w_first,
        b_first.reshape(1, -1),
        w_second,
        b_second.reshape(1, -1),
        w_third,
        b_third.reshape(1, -1),
    )


def solution(mesh):
    sizes = (mesh.shape["row"], mesh.shape["col"])
    both = ("row", "col")
    in_specs = (
        P(both, None, None),
        P(both),
        P(both, None, None),
        P(both),
        P(both),
        P(),
        P(),
        P(),
        P(),
        P(),
        P(),
        P(),
    )
    out_specs = (P(both, None, None), P(both, None))
    return jax.shard_map(
        functools.partial(body, sizes),
        mesh=mesh,
        in_specs=in_specs,
        out_specs=out_specs,
        check_vma=False,
    )
```

time: 324 us -> 235 us (0.73)
  Pallas kernels: 0 us -> 218 us
  waiting for transfers between devices: 187 us -> 0 us
  blocking collectives: 41.9 us -> 0 us
  matrix products: 37.3 us -> 0 us
  between operations: 15.6 us -> 1.99 us
  starting transfers between devices: 10.4 us -> 0 us
  other arithmetic: 12.6 us -> 3.91 us
  local copies, waits for them, and re-layouts: 18.3 us -> 10.6 us
    pallas_call x0 -> x2, Pallas kernels: none -> 218 us  [the longest x1 207 us: body(): pl.pallas_call(functools.partial(layer_kernel, sizes, bucket), out_shape=...]
    psum x1 -> x0, waiting for transfers between devices: 174 us -> none  [body(): lax.psum(readout_terms(graph_ids, pooled, READ_DEV * devices), ('row', 'c...]
    unnamed x1 -> x0, blocking collectives: 41.9 us -> none
    dot_general x4 -> x0, matrix products: 37.3 us -> none  [the longest x1 13.3 us: perceptron(): jnp.dot(hidden_two, w_third, preferred_element_type=jnp.float32) + b_third]
    all_to_all x2 -> x0, waiting for transfers between devices: 13.4 us -> none  [the longest x1 13.4 us: body(): lax.all_to_all(results[picked], ('row', 'col'), split_axis=0, concat_axis...]
    gather x2, local copies, waits for them, and re-layouts: 15.1 us -> 2.8 us  [the longest x1 2.02 us: body(): counts = node_counts[picked]]
    all_to_all x2 -> x0, starting transfers between devices: 10.4 us -> none  [the longest x1 5.97 us: body(): lax.all_to_all(results[picked], ('row', 'col'), split_axis=0, concat_axis...]
    reduce_sum x3 -> x1, other arithmetic: 9.08 us -> 0.18 us  [body(): source = jnp.sum(passed, axis=1)]
  transfers between devices with their start and end apart: 3 -> 0, of which waited for: 2 -> 0; matrix products, arithmetic and copies ran while one was open for 18% -> 0% of each run, Pallas kernels for 0% -> 0%
where the time goes in v1:
time: 235 us; the launch traced here: 234 us
  Pallas kernels  218 us (93%)
  local copies, waits for them, and re-layouts  10.6 us (5%)
  other arithmetic  3.91 us (2%)
    pallas_call x1, Pallas kernels, body(): pl.pallas_call(functools.partial(layer_kernel, sizes, bucket), out_shape=...  207 us
    pallas_call x1, Pallas kernels, gather_counts(): pl.pallas_call(functools.partial(gather_kernel, sizes), out_shape=jax.Sha...  11.4 us
    unnamed x6, local copies, waits for them, and re-layouts  5.26 us

profile of v1, /device:TPU:0, one launch (start us, length us, event | category | flops | bytes accessed | tf_op | source)
XLA Modules:
  0.0 234.5 jit_solution(2018111767653683467)
XLA Ops:
  0.6 0.0 copy-start
  1.9 0.5 broadcast_in_dim.7.own_ref
  2.5 11.4 %gather_counts.1 = s32[32,1,128]{2,1,0:T(1,128)} custom-call(s32[1,1,128]{2,1,0:T(1,128)} %broadcast_in_dim.7.own_ref), custom_call_target="tpu_custom_call" | custom-call | tf_op jit(solution)/shard_map/gather_counts/pallas_call | solution.py:72
  13.9 1.4 slice_reduce_fusion
  15.2 0.1 reduce-window.8
  15.3 0.1 reduce
  15.4 0.6 dynamic_slice.3
  16.0 0.2 fusion
  16.2 0.5 fusion.17.arrival_ref
  16.7 0.7 fusion.15
  17.4 1.2 fusion.9.picked_ref
  18.6 0.0 copy-done
  18.6 0.8 gather_fusion.1
  19.4 2.0 gather_fusion
  21.4 1.2 compare_select_fusion.8.ids_ref
  22.6 206.7 %gin_layer.1 = (bf16[32,128,512]{2,1,0:T(8,128)(2,1)}, f32[8,512]{1,0:T(8,128)}) custom-call(s32[64]{0:T(128)} %fusion.9.picked_ref, s32[64]{0:T(128)} %gather_fusion, s32[32]{0:T(128)} %fusion.17.arrival_ref, f32[1]{0:T(128)S(6)} %copy.20.weight_ref, bf16[64,128,512]{2,1,0:T(8,128)(2,1)} %features_ref.1, s32[64,2,256]{2,1,0:T(2,128)} %edges_ref.1, ...), custom_call_target="tpu_custom_call" | custom-call | tf_op jit(solution)/shard_map/gin_layer/pallas_call | solution.py:280
  229.2 0.0 copy-start.1
  229.2 4.6 %copy.21 = bf16[32,128,512]{2,1,0:T(8,128)(2,1)} copy(bf16[32,128,512]{2,1,0:T(8,128)(2,1)} %get-tuple-element.8) | data formatting | bytes 8388608
  233.9 0.0 copy-done.1
  233.9 0.6 copy.22
  (3 shorter events, 0.0 us)
Async XLA Ops:
  0.6 18.0 %copy-start = (s32[64]{0:T(128)S(1)}, s32[64]{0:T(128)}, u32[]{:S(2)}) copy-start(s32[64]{0:T(128)} %param.15) | copy-start | bytes 772
  229.2 4.7 %copy-start.1 = (f32[8,512]{1,0:T(8,128)S(1)}, f32[8,512]{1,0:T(8,128)}, u32[]{:S(2)}) copy-start(f32[8,512]{1,0:T(8,128)} %get-tuple-element.9) | copy-start | bytes 49156

commit v2 on v1

--- a/solution.py
+++ b/solution.py
@@ -10,6 +10,9 @@
 MESH = pl.DeviceIdType.MESH
 VMEM = pl.BlockSpec(memory_space=pltpu.VMEM)
 SMEM = pl.BlockSpec(memory_space=pltpu.SMEM)
+PLANES = 4
+UNIT = 16
+CLASSES = (2, 3, 1, 0)
 
 
 def partners(step, sizes):
@@ -66,12 +69,13 @@
     lax.fori_loop(1, devices, finish, 0)
 
 
-def gather_counts(live_graphs, sizes):
+def gather_counts(node_counts, live_graphs, sizes):
     devices = sizes[0] * sizes[1]
-    own = jnp.broadcast_to(live_graphs.reshape(1, 1, 1), (1, 1, 128))
+    own = jnp.concatenate([node_counts, live_graphs])
+    own = jnp.pad(own, (0, -own.shape[0] % 128)).reshape(1, 1, -1)
     every = pl.pallas_call(
         functools.partial(gather_kernel, sizes),
-        out_shape=jax.ShapeDtypeStruct((devices, 1, 128), jnp.int32),
+        out_shape=jax.ShapeDtypeStruct((devices, 1, own.shape[2]), jnp.int32),
         in_specs=[VMEM],
         out_specs=VMEM,
         scratch_shapes=[
@@ -81,7 +85,7 @@
         compiler_params=pltpu.CompilerParams(collective_id=0, has_side_effects=True),
         name="gather_counts",
     )(own)
-    return every[:, 0, 0]
+    return every[:, 0, :]
 
 
 def layer_kernel(
@@ -177,7 +181,7 @@
             + b_third_ref[...]
         )
         for j in range(bucket):
-            count = counts_ref[target * bucket + j]
+            count = counts_ref[picked_ref[target * bucket + j]]
             rows = jnp.where(node_index < count, result[j * block : (j + 1) * block], 0.0)
             rows = rows.astype(jnp.bfloat16)
             store(j, rows)
@@ -236,6 +240,236 @@
     def place(slot, carry):
         which = arrival_ref[slot]
         out_ref[slot] = arrived[which // bucket, which % bucket]
+        return carry
+
+    lax.fori_loop(0, out_ref.shape[0], place, 0)
+
+
+def relay_kernel(
+    sizes,
+    bucket,
+    units,
+    table_ref,
+    counts_ref,
+    weight_ref,
+    features_ref,
+    edges_ref,
+    ids_ref,
+    w_first_ref,
+    b_first_ref,
+    w_second_ref,
+    b_second_ref,
+    w_third_ref,
+    b_third_ref,
+    out_ref,
+    readout_ref,
+    sent,
+    arrived_a,
+    arrived_b,
+    arrived_c,
+    arrived_d,
+    packed,
+    unpacked,
+    pooled,
+    terms,
+    terms_in,
+    send_sem,
+    recv_sem,
+    relay_send_sem,
+    relay_recv_sem,
+    terms_send_sem,
+    terms_recv_sem,
+):
+    rows_n, cols_n = sizes
+    devices = rows_n * cols_n
+    width = cols_n // PLANES
+    in_plane = rows_n * width
+    read_rows = readout_ref.shape[0]
+    block, hidden = features_ref.shape[1:]
+    parts = block // UNIT
+    slots = devices * bucket
+    pack_at = slots
+    base_at = pack_at + PLANES * units
+    size_at = base_at + out_ref.shape[0]
+    arrived = (arrived_a, arrived_b, arrived_c, arrived_d)
+    row, col = lax.axis_index("row"), lax.axis_index("col")
+    me = row * cols_n + col
+    plane, lane = col // width, col % width
+    own_place = row * width + lane
+    barrier = greet(sizes)
+
+    def other_plane(k):
+        return (plane // 2 + k // 2) % 2 * 2 + (plane % 2 + k % 2) % 2
+
+    def neighbour_at(step):
+        to_row, to_lane = (row + step // width) % rows_n, (lane + step % width) % width
+        from_row = (row + rows_n - step // width) % rows_n
+        from_lane = (lane + width - step % width) % width
+        return (to_row, plane * width + to_lane), to_row, to_lane, from_row * width + from_lane
+
+    def graph_copy(number, k, step, place):
+        where, _, _, _ = neighbour_at(step)
+        return pltpu.make_async_remote_copy(
+            src_ref=sent.at[number * in_plane + step],
+            dst_ref=arrived[number].at[pl.ds(place * (bucket * parts), bucket * parts)],
+            send_sem=send_sem.at[number * in_plane + step],
+            recv_sem=recv_sem.at[number * in_plane + step],
+            device_id=where,
+            device_id_type=MESH,
+        )
+
+    def relay_copy(number, k, to_plane, from_plane):
+        return pltpu.make_async_remote_copy(
+            src_ref=packed.at[number],
+            dst_ref=unpacked.at[pl.ds(from_plane * units, units)],
+            send_sem=relay_send_sem.at[number],
+            recv_sem=relay_recv_sem.at[number],
+            device_id=(row, to_plane * width + lane),
+            device_id_type=MESH,
+        )
+
+    def terms_copy(step, target, slot):
+        where, _, _ = partners(step, sizes)
+        return pltpu.make_async_remote_copy(
+            src_ref=terms.at[target],
+            dst_ref=terms_in.at[slot],
+            send_sem=terms_send_sem.at[step],
+            recv_sem=terms_recv_sem.at[step],
+            device_id=where,
+            device_id_type=MESH,
+        )
+
+    node_rows = lax.broadcasted_iota(jnp.int32, (block, edges_ref.shape[2]), 0)
+    node_index = lax.broadcasted_iota(jnp.int32, (block, hidden), 0)
+
+    def compute(target, store):
+        blends = []
+        for j in range(bucket):
+            graph = table_ref[target * bucket + j]
+            features = features_ref[graph]
+            edges = edges_ref[graph]
+            sources = (node_rows == edges[0:1, :]).astype(jnp.float32).astype(jnp.bfloat16)
+            targets = (node_rows == edges[1:2, :]).astype(jnp.float32).astype(jnp.bfloat16)
+            adjacency = lax.dot_general(
+                targets,
+                sources,
+                (((1,), (1,)), ((), ())),
+                preferred_element_type=jnp.float32,
+            ).astype(jnp.bfloat16)
+            neighbour = jnp.dot(adjacency, features, preferred_element_type=jnp.float32)
+            blends.append(
+                (weight_ref[0] * features.astype(jnp.float32) + neighbour).astype(jnp.bfloat16)
+            )
+        blended = jnp.concatenate(blends, axis=0) if bucket > 1 else blends[0]
+        hidden_one = jnp.maximum(
+            jnp.dot(blended, w_first_ref[...], preferred_element_type=jnp.float32)
+            + b_first_ref[...],
+            0.0,
+        ).astype(jnp.bfloat16)
+        hidden_two = jnp.maximum(
+            jnp.dot(hidden_one, w_second_ref[...], preferred_element_type=jnp.float32)
+            + b_second_ref[...],
+            0.0,
+        ).astype(jnp.bfloat16)
+        result = (
+            jnp.dot(hidden_two, w_third_ref[...], preferred_element_type=jnp.float32)
+            + b_third_ref[...]
+        )
+        for j in range(bucket):
+            count = counts_ref[table_ref[target * bucket + j]]
+            rows = jnp.where(node_index < count, result[j * block : (j + 1) * block], 0.0)
+            rows = rows.astype(jnp.bfloat16)
+            store(j, rows.reshape(parts, UNIT, hidden))
+            total = jnp.sum(rows.astype(jnp.float32), axis=0, keepdims=True)
+            pooled[target * bucket + j] = total / jnp.full((1, hidden), count).astype(jnp.float32)
+
+    def first_stage(number, k):
+        def compute_and_send(step, carry):
+            _, to_row, to_lane, _ = neighbour_at(step)
+
+            def store(j, rows):
+                sent[number * in_plane + step, pl.ds(j * parts, parts)] = rows
+
+            compute(to_row * cols_n + other_plane(k) * width + to_lane, store)
+            graph_copy(number, k, step, own_place).start()
+            return carry
+
+        lax.fori_loop(1, in_plane, compute_and_send, 0)
+
+        def store_own(j, rows):
+            arrived[number][pl.ds((own_place * bucket + j) * parts, parts)] = rows
+
+        compute(row * cols_n + other_plane(k) * width + lane, store_own)
+
+    def second_stage(number, k):
+        def finish(step, carry):
+            _, _, _, source = neighbour_at(step)
+            graph_copy(number, k, step, own_place).wait_send()
+            graph_copy(number, k, step, source).wait_recv()
+            return carry
+
+        lax.fori_loop(1, in_plane, finish, 0)
+        to_plane = other_plane(k)
+
+        def pack(step, carry):
+            for n in range(8):
+                unit = step * 8 + n
+                value = arrived[number][table_ref[pack_at + to_plane * units + unit]]
+                if k == 0:
+                    unpacked[plane * units + unit] = value
+                else:
+                    packed[number, unit] = value
+            return carry
+
+        lax.fori_loop(0, units // 8, pack, 0)
+        if k != 0:
+            relay_copy(number, k, to_plane, plane).start()
+
+    pl.semaphore_wait(barrier, devices - 1)
+    for number, k in enumerate(CLASSES):
+        first_stage(number, k)
+        if number > 0:
+            second_stage(number - 1, CLASSES[number - 1])
+
+    keys = lax.broadcasted_iota(jnp.int32, (devices * read_rows, slots), 0)
+    members = (keys == ids_ref[...]).astype(jnp.float32)
+    all_terms = jnp.dot(
+        members,
+        pooled[...].reshape(slots, hidden),
+        precision=lax.Precision.HIGHEST,
+        preferred_element_type=jnp.float32,
+    )
+    terms[...] = all_terms.reshape(devices, read_rows, hidden)
+
+    def send_terms(step, carry):
+        _, target, _ = partners(step, sizes)
+        terms_copy(step, target, me).start()
+        return carry
+
+    lax.fori_loop(1, devices, send_terms, 0)
+    terms_in[me] = terms[me]
+    second_stage(PLANES - 1, CLASSES[PLANES - 1])
+
+    def finish_terms(step, carry):
+        _, target, source = partners(step, sizes)
+        terms_copy(step, target, me).wait_send()
+        terms_copy(step, target, source).wait_recv()
+        return carry
+
+    lax.fori_loop(1, devices, finish_terms, 0)
+    readout_ref[...] = jnp.sum(terms_in[...], axis=0)
+    for number, k in enumerate(CLASSES):
+        if k != 0:
+            relay_copy(number, k, other_plane(k), plane).wait_send()
+            relay_copy(number, k, other_plane(k), other_plane(k)).wait_recv()
+
+    def place(slot, carry):
+        base = table_ref[base_at + slot]
+        size = table_ref[size_at + slot]
+        for part in range(parts):
+            value = unpacked[jnp.minimum(base + part, PLANES * units - 1)]
+            value = jnp.where(jnp.full((UNIT, hidden), size) > part, value, jnp.zeros_like(value))
+            out_ref[slot, pl.ds(part * UNIT, UNIT), :] = value
         return carry
 
     lax.fori_loop(0, out_ref.shape[0], place, 0)
@@ -256,58 +490,156 @@
     w_third,
     b_third,
 ):
-    devices = sizes[0] * sizes[1]
+    rows_n, cols_n = sizes
+    devices = rows_n * cols_n
+    width = cols_n // PLANES
+    in_plane = rows_n * width
     capacity, block, hidden = node_features.shape
+    parts = block // UNIT
     graphs_out = capacity // 2
     read_rows = 8
     bucket = (capacity + devices - 1) // devices
+    slots_n = devices * bucket
+    units = graphs_out * parts * 5 // (PLANES * 4)
     own_count = live_graphs[0]
-    me = lax.axis_index(("row", "col"))
-    every_count = gather_counts(live_graphs, sizes)
-    inclusive = jnp.cumsum(every_count)
+    row, col = lax.axis_index("row"), lax.axis_index("col")
+    plane, lane = col // width, col % width
+    me = row * cols_n + col
+    every = gather_counts(node_counts, live_graphs, sizes)
+    every_count = every[:, capacity]
+    earlier = jnp.arange(devices)[:, None] >= jnp.arange(devices)[None, :]
+    inclusive = jnp.sum(jnp.where(earlier, every_count[None, :], 0), axis=1)
     offsets = inclusive - every_count
-    offset = offsets[me]
-    slots = lax.broadcasted_iota(jnp.int32, (devices * bucket,), 0)
+    offset = jnp.sum(jnp.where(jnp.arange(devices) == me, offsets, 0))
+    slots = lax.broadcasted_iota(jnp.int32, (slots_n,), 0)
     within = (slots // bucket - offset) % devices + slots % bucket * devices
     picked = jnp.minimum(within, capacity - 1)
-    counts = node_counts[picked]
-    graph_ids = jnp.where(within < own_count, readout_ids[picked], -1)
+    choose = picked[:, None] == jnp.arange(capacity)[None, :]
+    picked_ids = jnp.sum(jnp.where(choose, readout_ids[None, :], 0), axis=1)
+    graph_ids = jnp.where(within < own_count, picked_ids, -1).reshape(1, -1)
     number = lax.broadcasted_iota(jnp.int32, (graphs_out,), 0) * devices + me
     passed = (inclusive[None, :] <= number[:, None]).astype(jnp.int32)
     source = jnp.sum(passed, axis=1)
     start = jnp.sum(passed * every_count[None, :], axis=1)
-    arrival = source * bucket + (number - start) // devices
-    return pl.pallas_call(
-        functools.partial(layer_kernel, sizes, bucket),
-        out_shape=(
-            jax.ShapeDtypeStruct((graphs_out, block, hidden), jnp.bfloat16),
-            jax.ShapeDtypeStruct((read_rows, hidden), jnp.float32),
-        ),
-        in_specs=[SMEM] * 4 + [VMEM] * 9,
-        out_specs=(VMEM, VMEM),
-        scratch_shapes=[
-            pltpu.VMEM((devices, bucket, block, hidden), jnp.bfloat16),
-            pltpu.VMEM((devices, bucket, block, hidden), jnp.bfloat16),
-            pltpu.VMEM((devices * bucket, 1, hidden), jnp.float32),
-            pltpu.VMEM((devices, read_rows, hidden), jnp.float32),
-            pltpu.VMEM((devices, read_rows, hidden), jnp.float32),
-            pltpu.SemaphoreType.DMA((devices,)),
-            pltpu.SemaphoreType.DMA((devices,)),
-            pltpu.SemaphoreType.DMA((devices,)),
-            pltpu.SemaphoreType.DMA((devices,)),
-        ],
-        compiler_params=pltpu.CompilerParams(
-            collective_id=1, has_side_effects=True, vmem_limit_bytes=60 * 1024 * 1024
-        ),
-        name="gin_layer",
-    )(
-        picked,
-        counts,
+    turn = (number - start) // devices
+
+    index = jnp.arange(capacity)[None, :]
+    sizes_all = jnp.where(
+        index < every_count[:, None], (every[:, :capacity] + (UNIT - 1)) // UNIT, 0
+    )
+    dests = (offsets[:, None] + index) % devices
+    by_dest = jnp.sum(
+        jnp.where(dests[:, :, None] == jnp.arange(devices), sizes_all[:, :, None], 0), axis=1
+    )
+    plane_load = jnp.sum(by_dest.reshape(rows_n, PLANES, width, devices), axis=(0, 2))
+    fits = jnp.max(plane_load) <= units
+
+    turns = jnp.arange(bucket)[:, None] == index // devices
+
+    def by_plane(values):
+        values = values.reshape(rows_n, PLANES, width, capacity)
+        return jnp.swapaxes(values, 0, 1).reshape(PLANES, in_plane, capacity)
+
+    plane_sizes, plane_dests = by_plane(sizes_all), by_plane(dests)
+    own_sizes = lax.dynamic_index_in_dim(plane_sizes, plane, 0, keepdims=False)
+    own_dests = lax.dynamic_index_in_dim(plane_dests, plane, 0, keepdims=False)
+
+    def slot_sizes(values, wanted):
+        chosen = wanted[:, :, None, :] & turns
+        return jnp.sum(jnp.where(chosen, values[:, :, None, :], 0), axis=3).reshape(PLANES, -1)
+
+    relay_dests = row * cols_n + jnp.arange(PLANES) * width + lane
+    relay_sizes = slot_sizes(own_sizes[None], own_dests[None] == relay_dests[:, None, None])
+    final_sizes = slot_sizes(plane_sizes, plane_dests == me)
+    places = in_plane * bucket
+    before = jnp.arange(places)[:, None] >= jnp.arange(places)[None, :]
+
+    def ends(values):
+        return jnp.sum(jnp.where(before, values[:, None, :], 0), axis=2)
+
+    done = ends(relay_sizes)[:, None, :] <= jnp.arange(units)[None, :, None]
+    slot_of = jnp.minimum(jnp.sum(done.astype(jnp.int32), axis=2), places - 1)
+    part_of = jnp.arange(units) - jnp.sum(jnp.where(done, relay_sizes[:, None, :], 0), axis=2)
+    pack = slot_of * parts + jnp.clip(part_of, 0, parts - 1)
+    starts = ends(final_sizes) - final_sizes + jnp.arange(PLANES)[:, None] * units
+    source_row, source_col = source // cols_n, source % cols_n
+    place = (source_row * width + source_col % width) * bucket + turn
+    place = source_col // width * places + place
+    match = place[:, None] == jnp.arange(PLANES * places)[None, :]
+    base = jnp.sum(jnp.where(match, starts.reshape(1, -1), 0), axis=1)
+    size = jnp.sum(jnp.where(match, final_sizes.reshape(1, -1), 0), axis=1)
+    table = jnp.concatenate([picked, pack.reshape(-1), base, size]).astype(jnp.int32)
+    arrival = (source * bucket + turn).astype(jnp.int32)
+
+    out_shape = (
+        jax.ShapeDtypeStruct((graphs_out, block, hidden), jnp.bfloat16),
+        jax.ShapeDtypeStruct((read_rows, hidden), jnp.float32),
+    )
+    pooled_scratch = [
+        pltpu.VMEM((slots_n, 1, hidden), jnp.float32),
+        pltpu.VMEM((devices, read_rows, hidden), jnp.float32),
+        pltpu.VMEM((devices, read_rows, hidden), jnp.float32),
+    ]
+
+    def semaphores(count):
+        return [pltpu.SemaphoreType.DMA((count,)), pltpu.SemaphoreType.DMA((count,))]
+
+    def relayed(*operands):
+        table, _, node_counts = operands[:3]
+        graphs = pltpu.VMEM((in_plane * bucket * parts, UNIT, hidden), jnp.bfloat16)
+        return pl.pallas_call(
+            functools.partial(relay_kernel, sizes, bucket, units),
+            out_shape=out_shape,
+            in_specs=[SMEM] * 3 + [VMEM] * 9,
+            out_specs=(VMEM, VMEM),
+            scratch_shapes=[
+                pltpu.VMEM((devices, bucket * parts, UNIT, hidden), jnp.bfloat16),
+                graphs,
+                graphs,
+                graphs,
+                graphs,
+                pltpu.VMEM((PLANES - 1, units, UNIT, hidden), jnp.bfloat16),
+                pltpu.VMEM((PLANES * units, UNIT, hidden), jnp.bfloat16),
+            ]
+            + pooled_scratch
+            + semaphores(devices)
+            + semaphores(PLANES)
+            + semaphores(devices),
+            compiler_params=pltpu.CompilerParams(
+                collective_id=2, has_side_effects=True, vmem_limit_bytes=61 * 1024 * 1024
+            ),
+            name="gin_relay",
+        )(table, node_counts, *operands[3:])
+
+    def direct(*operands):
+        table, arrival, node_counts = operands[:3]
+        graphs = pltpu.VMEM((devices, bucket, block, hidden), jnp.bfloat16)
+        return pl.pallas_call(
+            functools.partial(layer_kernel, sizes, bucket),
+            out_shape=out_shape,
+            in_specs=[SMEM] * 4 + [VMEM] * 9,
+            out_specs=(VMEM, VMEM),
+            scratch_shapes=[graphs, graphs]
+            + pooled_scratch
+            + semaphores(devices)
+            + semaphores(devices),
+            compiler_params=pltpu.CompilerParams(
+                collective_id=1, has_side_effects=True, vmem_limit_bytes=60 * 1024 * 1024
+            ),
+            name="gin_direct",
+        )(table[:slots_n], node_counts, arrival, *operands[3:])
+
+    return lax.cond(
+        fits,
+        relayed,
+        direct,
+        table,
         arrival,
+        node_counts,
         self_weight,
         node_features,
         edge_list,
-        graph_ids.reshape(1, -1),
+        graph_ids,
         w_first,
         b_first.reshape(1, -1),
         w_second,

time: 235 us -> 197 us (0.84)
  Pallas kernels: 218 us -> 179 us
  other arithmetic: 3.91 us -> 8.01 us
  local copies, waits for them, and re-layouts: 10.6 us -> 7.94 us
    pallas_call x1, Pallas kernels: 207 us -> 167 us  [relayed(): pl.pallas_call(functools.partial(relay_kernel, sizes, bucket, units), out...]
    reduce_sum x1 -> x10, other arithmetic: 0.18 us -> 3.28 us  [the longest x1 0.83 us: body(): picked_ids = jnp.sum(jnp.where(choose, readout_ids[None, :], 0), axis=1)]
    gather x2 -> x0, local copies, waits for them, and re-layouts: 2.8 us -> none  [the longest x1 2.02 us: body(): counts = node_counts[picked]]
    unnamed x6 -> x2, local copies, waits for them, and re-layouts: 5.26 us -> 5.24 us
where the time goes in v2:
time: 197 us
  Pallas kernels  179 us (91%)
  other arithmetic  8.01 us (4%)
  local copies, waits for them, and re-layouts  7.94 us (4%)
  between operations  2.11 us (1%)
    pallas_call x1, Pallas kernels, relayed(): pl.pallas_call(functools.partial(relay_kernel, sizes, bucket, units), out...  167 us
    pallas_call x1, Pallas kernels, gather_counts(): pl.pallas_call(functools.partial(gather_kernel, sizes), out_shape=jax.Sha...  11.4 us
    unnamed x2, local copies, waits for them, and re-layouts  5.24 us

profile of v2, /device:TPU:0, one launch (start us, length us, event | category | flops | bytes accessed | tf_op | source)
XLA Modules:
  0.0 196.8 jit_solution(12801541488653083935)
XLA Ops:
  1.3 0.7 pad_add_fusion.1
  2.0 0.5 pad_bitcast_fusion.own_ref
  2.6 0.1 add.296
  2.6 0.1 add.297
  2.7 11.4 %gather_counts.1 = s32[32,1,128]{2,1,0:T(1,128)} custom-call(s32[1,1,128]{2,1,0:T(1,128)} %pad_bitcast_fusion.own_ref), custom_call_target="tpu_custom_call" | custom-call | tf_op jit(solution)/shard_map/gather_counts/pallas_call | solution.py:76
  14.1 0.9 slice_reduce_fusion
  15.0 0.1 select_reduce_fusion.9
  15.1 0.6 fusion.21
  15.8 0.2 fusion.1
  16.0 0.7 and_select_fusion.6
  16.7 0.8 select_reduce_fusion.6
  17.5 0.7 compare_select_fusion.5
  18.2 0.1 copy.33
  18.3 0.9 subtract_reduce_fusion
  19.2 0.1 add.275
  19.3 0.1 copy.35
  19.4 0.1 copy.36
  19.5 0.8 add_select_fusion.2
  20.3 0.6 select_reduce_fusion
  21.0 0.6 reduce_max.9
  22.3 0.1 add_select_fusion
  22.4 0.1 broadcast_compare_fusion
  22.5 0.4 select_reduce_fusion.5
  22.9 0.1 copy.38
  22.9 0.1 copy.39
  23.0 0.1 copy.41
  23.1 0.1 copy.42
  23.2 0.2 select_reduce_fusion.4
  23.4 0.1 convert_reduce_fusion
  23.6 0.1 add.289
  23.6 0.1 reduce_sum.156
  23.7 0.1 copy.43
  23.8 0.1 reshape.418
  23.9 0.2 select_reduce_fusion.8
  24.1 0.1 pad_add_fusion
  24.2 167.3 %conditional.1 = ((bf16[32,128,512]{2,1,0:T(8,128)(2,1)}, f32[8,512]{1,0:T(8,128)S(1)})) conditional(s32[]{:T(128)} %convert_element_type.9, (s32[32]{0:T(128)S(1)}, s32[32]{0:T(128)S(1)}, s32[32]{0:T(128)S(1)}, pred[32]{0:T(512)(128)(4,1)S(1)}, s32[32]{0:T(128)S(1)}, /*index=5*/s32[32]{0:T(128)S(1)}, s32[64]{0:T(128)S(1)}, s32[64]{0:T(128)}, ...), branch_computations={%region_16.17_spmd, %region_17.18_spmd} | conditional | flops 320 | bytes 808 | solution.py:632
  24.2 167.3 %gin_relay.1 = (bf16[32,128,512]{2,1,0:T(8,128)(2,1)}, f32[8,512]{1,0:T(8,128)S(1)}) custom-call(s32[448]{0:T(512)S(1)} %get-tuple-element.96.table_ref, s32[64]{0:T(128)} %get-tuple-element.97.counts_ref, f32[1]{0:T(128)} %get-tuple-element.98.weight_ref, bf16[64,128,512]{2,1,0:T(8,128)(2,1)} %get-tuple-element.99.features_ref, ...), custom_call_target="tpu_custom_call" | custom-call | tf_op jit(solution)/shard_map/cond/branch_1_fun/gin_relay/pallas_call | solution.py:590
  191.5 4.6 %copy.53 = bf16[32,128,512]{2,1,0:T(8,128)(2,1)} copy(bf16[32,128,512]{2,1,0:T(8,128)(2,1)} %get-tuple-element.142) | data formatting | bytes 8388608
  196.2 0.6 copy.54
  (15 shorter events, 0.1 us)
